TPU v7x, 32 devices: a whole 2x2x4 slice. The times are simulated.
32 devices in a mesh: gy: 4 (over z), gz: 8 (over y, x, core).
Axes of the slice: x: 2, y: 2, z: 4, core: 2. Of those that a mesh axis runs over, the one named last changes fastest.
Arguments:
- velocity: float32 [3, 32, 64, 128], P(None, 'gy', 'gz'), may hold values from -6 to 6
- offsets: float32 [3, 32768], P(None, ('gy', 'gz')), may hold values from 2 to 6
- marker_slot: int32 [32768], P(('gy', 'gz')), may hold values from 0 to 1
- fibre_links: int32 [2, 32768], P(None, ('gy', 'gz')), may hold values from 0 to 127
- block_owner: int32 [256, 1], P(('gy', 'gz')), may hold values from 0 to 7; in each aligned block of 8 rows (0 to 7, 8 to 15, ...) at most 2 rows name the same one
- block_tiles: int32 [256, 2], P(('gy', 'gz')), may hold values from 0 to 15
Outputs:
- new_velocity: float32 [3, 32, 64, 128], P(None, 'gy', 'gz')
- marker_velocity: float32 [3, 32768], P(None, ('gy', 'gz'))
Inputs may be any that keep to these rules, and one draw needn't show every extreme that they name: `block_owner`: of the 8 blocks of one device, at most 2 name the same index; in some device one index is named exactly 2 times. `block_tiles`: tiles are numbered (y, z, x) row-major over the owner's tiles of 8 cells a side; two slots of a block may name the same tile. `fibre_links`: A marker may be its own partner.
All inputs are finite; a program needn't handle non-finite values.
Results may differ from a plain program's by a relative error of at most 0.0003.
Values sent between devices are 32-bit elements; how exact they have to be, the bound alone decides.
A program may use at most 64 MiB of HBM per device.

v0:
```python
import math

import jax
import jax.numpy as jnp
from jax import lax
from jax.sharding import PartitionSpec as P

BLOCK = 128
TILE_SIDE = 8
STEPS = 2


TENSION = 1.0
VISCOUS = 0.125
FORCING = 0.5
HIGHEST = lax.Precision.HIGHEST


def padded_2(cells, sides, width):
    for axis, dim in sides:
        count = lax.axis_size(axis)
        head = lax.slice_in_dim(cells, 0, width, axis=dim)
        tail = lax.slice_in_dim(cells, cells.shape[dim] - width, cells.shape[dim], axis=dim)
        cells = jnp.concatenate(
            [
                lax.ppermute(tail, axis, [(i, (i + 1) % count) for i in range(count)]),
                cells,
                lax.ppermute(head, axis, [((i + 1) % count, i) for i in range(count)]),
            ],
            axis=dim,
        )
    return cells


def kernel_weights(offset_rows):
    cells = jnp.arange(TILE_SIDE).astype(offset_rows.dtype)
    distance = cells[None, :, None] - offset_rows[:, None, :]
    bump = (1.0 + jnp.cos(0.5 * math.pi * distance)) * 0.25
    return jnp.where(jnp.abs(distance) < 2.0, bump, jnp.zeros_like(bump))


def slot_masks(slot_rows, slot_count, dtype):
    slot_ids = jnp.arange(slot_count)
    return (slot_rows[:, None, :] == slot_ids[None, :, None]).astype(dtype)


def kernel_planes(offset_rows):
    along_y = kernel_weights(offset_rows[:, 0])
    along_z = kernel_weights(offset_rows[:, 1])
    along_x = kernel_weights(offset_rows[:, 2])
    count = offset_rows.shape[0]
    plane = (along_z[:, :, None, :] * along_x[:, None, :, :]).reshape(
        count, TILE_SIDE * TILE_SIDE, offset_rows.shape[2]
    )
    return (along_y, plane)


def spread_terms(force_rows, offset_rows, slot_rows, slot_count):
    masks = slot_masks(slot_rows, slot_count, force_rows.dtype)
    along_y, plane = kernel_planes(offset_rows)
    lifted = (
        masks[:, :, None, None, :] * force_rows[:, None, :, None, :] * along_y[:, None, None, :, :]
    )
    terms = jnp.einsum("bkcjm,bnm->bkcjn", lifted, plane, precision=HIGHEST)
    return terms.reshape(force_rows.shape[0], slot_count, 3 * TILE_SIDE**3)


def interpolate(tile_values, offset_rows, slot_rows, slot_count):
    masks = slot_masks(slot_rows, slot_count, tile_values.dtype)
    along_y, plane = kernel_planes(offset_rows)
    count = tile_values.shape[0]
    shaped = tile_values.reshape(count, slot_count, 3, TILE_SIDE, TILE_SIDE * TILE_SIDE)
    partial_sums = jnp.einsum("bkcjn,bnm->bkcjm", shaped, plane, precision=HIGHEST)
    return jnp.sum(
        partial_sums * along_y[:, None, None, :, :] * masks[:, :, None, None, :], axis=(1, 3)
    )


def place_markers(anchor, offset_rows, slot_rows):
    masks = slot_masks(slot_rows, anchor.shape[1], offset_rows.dtype)
    return jnp.sum(masks[:, :, None, :] * anchor[:, :, :, None], axis=1) + offset_rows


def fibre_force(position, link_rows):
    total = jnp.zeros_like(position)
    for partner_side in range(2):
        partner_index = jnp.broadcast_to(link_rows[partner_side][:, None, :], position.shape)
        delta = jnp.take_along_axis(position, partner_index, axis=2) - position
        length = jnp.sqrt(jnp.sum(delta * delta, axis=1, keepdims=True))
        total = total + TENSION * delta / jnp.maximum(length, 1.0)
    return total


def tile_anchor(tile_ids, row_index, column_ids, span_y, span_z, tiles_z, tiles_x):
    tile_y = tile_ids // (tiles_z * tiles_x)
    tile_z = tile_ids // tiles_x % tiles_z
    tile_x = tile_ids % tiles_x
    return jnp.stack(
        [
            row_index * span_y + tile_y * TILE_SIDE,
            column_ids * span_z + tile_z * TILE_SIDE,
            tile_x * TILE_SIDE,
        ],
        axis=-1,
    ).astype(jnp.float32)


def to_tiles(field):
    comps, span_y, span_z, span_x = field.shape
    side = TILE_SIDE
    shaped = field.reshape(comps, span_y // side, side, span_z // side, side, span_x // side, side)
    shaped = shaped.transpose(1, 3, 5, 0, 2, 4, 6)
    return shaped.reshape(span_y // side * (span_z // side) * (span_x // side), comps * side**3)


def from_tiles(tiles, span_y, span_z, span_x):
    side = TILE_SIDE
    shaped = tiles.reshape(span_y // side, span_z // side, span_x // side, 3, side, side, side)
    return shaped.transpose(3, 0, 4, 1, 5, 2, 6).reshape(3, span_y, span_z, span_x)


def margin_laplace(padded):
    centre = padded[:, 1:-1, 1:-1]
    walled = jnp.pad(centre, ((0, 0), (0, 0), (0, 0), (1, 1)))
    beside_all = (
        padded[:, 2:, 1:-1] + padded[:, :-2, 1:-1] + padded[:, 1:-1, 2:] + padded[:, 1:-1, :-2]
    )
    return beside_all + walled[..., 2:] + walled[..., :-2] - 6.0 * centre


def local(velocity, offsets, marker_slot, fibre_links, block_owner, block_tiles):
    block_count, slot_count = block_tiles.shape
    span_y, span_z, span_x = (velocity.shape[1], velocity.shape[2], velocity.shape[3])
    tiles_y = span_y // TILE_SIDE
    tiles_z = span_z // TILE_SIDE
    tiles_x = span_x // TILE_SIDE
    tile_count = tiles_y * tiles_z * tiles_x
    tile_len = 3 * TILE_SIDE**3
    peers = lax.axis_size("gz")
    capacity = max(2, 2 * block_count // peers)
    slot_total = peers * capacity
    owner_ids = block_owner[:, 0]
    offset_rows = offsets.reshape(3, block_count, BLOCK).transpose(1, 0, 2)
    slot_rows = marker_slot.reshape(block_count, BLOCK)
    link_rows = fibre_links.reshape(2, block_count, BLOCK)
    grid_row = lax.axis_index("gy")
    anchor = tile_anchor(
        block_tiles, grid_row, owner_ids[:, None], span_y, span_z, tiles_z, tiles_x
    )
    position = place_markers(anchor, offset_rows, slot_rows)
    force_rows = fibre_force(position, link_rows)
    owner_onehot = (owner_ids[:, None] == jnp.arange(peers)[None, :]).astype(jnp.int32)
    earlier = jnp.cumsum(owner_onehot, axis=0) - owner_onehot
    target = owner_ids * capacity + jnp.sum(earlier * owner_onehot, axis=1)
    pack_int = (jnp.arange(slot_total)[:, None] == target[None, :]).astype(jnp.int32)
    packing = pack_int.astype(jnp.float32)
    sent_tiles = jnp.sum(pack_int[:, :, None] * (block_tiles[None, :, :] + 1), axis=1) - 1
    terms = spread_terms(force_rows, offset_rows, slot_rows, slot_count)
    outgoing = jnp.einsum("sb,bkn->skn", packing, terms, precision=HIGHEST)
    arrived, arrived_tiles = (
        lax.all_to_all(outgoing, "gz", split_axis=0, concat_axis=0, tiled=True),
        lax.all_to_all(sent_tiles, "gz", split_axis=0, concat_axis=0, tiled=True),
    )
    flat_tiles = arrived_tiles.reshape(-1)
    selector = (jnp.arange(tile_count)[:, None] == flat_tiles[None, :]).astype(jnp.float32)
    force_tiles = jnp.dot(selector, arrived.reshape(-1, tile_len), precision=HIGHEST)
    spread = from_tiles(force_tiles, span_y, span_z, span_x)
    field = velocity
    for substep in range(STEPS):
        padded = padded_2(field, (("gy", 1), ("gz", 2)), 1)
        field = field + VISCOUS * margin_laplace(padded) + FORCING * spread
    velocity_tiles = to_tiles(field)
    valid = (arrived_tiles >= 0).astype(jnp.float32)
    tile_values = (
        jnp.take(velocity_tiles, jnp.maximum(arrived_tiles, 0), axis=0) * valid[:, :, None]
    )
    returned = lax.all_to_all(tile_values, "gz", split_axis=0, concat_axis=0, tiled=True)
    block_values = jnp.einsum("sb,skn->bkn", packing, returned, precision=HIGHEST)
    sampled = interpolate(block_values, offset_rows, slot_rows, slot_count)
    marker_velocity = sampled.transpose(1, 0, 2).reshape(3, block_count * BLOCK)
    return (field, marker_velocity)


def solution(mesh):
    return jax.shard_map(
        local,
        mesh=mesh,
        in_specs=(
            P(None, "gy", "gz", None),
            P(None, ("gy", "gz")),
            P(("gy", "gz")),
            P(None, ("gy", "gz")),
            P(("gy", "gz"), None),
            P(("gy", "gz"), None),
        ),
        out_specs=(P(None, "gy", "gz", None), P(None, ("gy", "gz"))),
        check_vma=False,
    )
```

profile of v0, /device:TPU:0, one launch (start us, length us, event | category | flops | bytes accessed | tf_op | source)
XLA Modules:
  0.0 93.8 jit_solution(5726888332569570480)
XLA Ops:
  0.6 0.7 fusion.70
  1.4 0.8 select_reduce_fusion
  3.0 0.7 broadcast_add_fusion.3
  4.4 5.2 %all-to-all-start = ((s32[8,2,2]{1,2,0:T(2,128)}), s32[8,2,2]{1,2,0:T(2,128)S(1)}, u32[]{:S(2)}, u32[]{:S(2)}) async-start(s32[8,2,2]{1,2,0:T(2,128)} %copy.81), calls=%async_computation | async-start | bytes 16384 | tf_op jit(solution)/shard_map/all_to_all | solution.py:162
  9.6 0.7 fusion.82
  10.4 1.6 %collective-permute-start.1 = (f32[3,1,8,128]{3,2,1,0:T(8,128)S(1)}, f32[3,1,8,128]{3,2,1,0:T(8,128)S(1)}, u32[]{:S(2)}, u32[]{:S(2)}) collective-permute-start(f32[3,1,8,128]{3,2,1,0:T(8,128)S(1)} %get-tuple-element.16), channel_id=1, source_target_pairs={{0,8},{8,16},{16,24},{24,0},{1,9},{9,17},{17,25},{25,1},{2,10},{10... | collective-permute-start | bytes 36872 | tf_op jit(solution)/shard_map/ppermute | solution.py:26
  11.9 2.2 %collective-permute-start = (f32[3,1,8,128]{3,2,1,0:T(8,128)S(1)}, f32[3,1,8,128]{3,2,1,0:T(8,128)S(1)}, u32[]{:S(2)}, u32[]{:S(2)}) collective-permute-start(f32[3,1,8,128]{3,2,1,0:T(8,128)S(1)} %get-tuple-element.15), channel_id=1, source_target_pairs={{8,0},{16,8},{24,16},{0,24},{9,1},{17,9},{25,17},{1,25},{10,2},{18... | collective-permute-start | bytes 36872 | tf_op jit(solution)/shard_map/ppermute | solution.py:28
  14.2 0.8 fusion.83
  15.8 0.7 compare_convert_fusion
  16.6 0.7 copy_add_fusion
  17.3 18.4 %gather_fusion.1 = f32[3072]{0:T(1024)S(1)} fusion(f32[8,3,128]{2,0,1:T(8,128)S(1)} %get-tuple-element.7, s32[3072]{0:T(1024)S(1)} %reshape.299), kind=kCustom, calls=%fused_computation.clone | custom fusion | bytes 61440 | tf_op jit(solution)/shard_map/jit(take_along_axis)/gather | solution.py:88
  35.9 18.5 %gather_fusion.2 = f32[3072]{0:T(1024)S(1)} fusion(f32[8,3,128]{2,0,1:T(8,128)S(1)} %get-tuple-element.7, s32[3072]{0:T(1024)S(1)} %reshape.304), kind=kCustom, calls=%fused_computation.1.clone | custom fusion | bytes 61440 | tf_op jit(solution)/shard_map/jit(take_along_axis)/gather | solution.py:88
  56.0 0.8 copy.91
  56.8 4.2 %all-to-all-start.1 = ((f32[16,2,1536]{2,1,0:T(2,128)}), f32[16,2,1536]{2,1,0:T(2,128)S(1)}, u32[]{:S(2)}, u32[]{:S(2)}) async-start(f32[16,2,1536]{2,1,0:T(2,128)} %copy.91), calls=%async_computation.1 | async-start | bytes 393216 | tf_op jit(solution)/shard_map/all_to_all | solution.py:161
  61.4 2.7 %collective-permute-start.2 = (f32[3,10,1,128]{3,2,1,0:T(1,128)S(1)}, f32[3,10,1,128]{3,2,1,0:T(1,128)S(1)}, u32[]{:S(2)}, u32[]{:S(2)}) collective-permute-start(f32[3,10,1,128]{3,2,1,0:T(1,128)S(1)} %get-tuple-element.11), channel_id=1, source_target_pairs={{1,0},{2,1},{3,2},{4,3},{5,4},{6,5},{7,6},{0,7},{9,8},{10,9},{11,1... | collective-permute-start | bytes 46088 | tf_op jit(solution)/shard_map/ppermute | solution.py:28
  64.1 3.1 %all-to-all-done.1 = f32[16,2,1536]{2,1,0:T(2,128)S(1)} async-done(((f32[16,2,1536]{2,1,0:T(2,128)}), f32[16,2,1536]{2,1,0:T(2,128)S(1)}, u32[]{:S(2)}, u32[]{:S(2)}) %all-to-all-start.1) | async-done | bytes 196640 | tf_op jit(solution)/shard_map/all_to_all | solution.py:161
  68.6 0.8 mul.237
  69.6 1.9 %collective-permute-start.4 = (f32[3,1,8,128]{3,2,1,0:T(8,128)S(1)}, f32[3,1,8,128]{3,2,1,0:T(8,128)S(1)}, u32[]{:S(2)}, u32[]{:S(2)}) collective-permute-start(f32[3,1,8,128]{3,2,1,0:T(8,128)S(1)} %get-tuple-element.14), channel_id=1, source_target_pairs={{8,0},{16,8},{24,16},{0,24},{9,1},{17,9},{25,17},{1,25},{10,2},{18... | collective-permute-start | bytes 36872 | tf_op jit(solution)/shard_map/ppermute | solution.py:28
  71.8 1.5 %collective-permute-done.4 = f32[3,1,8,128]{3,2,1,0:T(8,128)S(1)} collective-permute-done((f32[3,1,8,128]{3,2,1,0:T(8,128)S(1)}, f32[3,1,8,128]{3,2,1,0:T(8,128)S(1)}, u32[]{:S(2)}, u32[]{:S(2)}) %collective-permute-start.4) | collective-permute-done | bytes 12320 | tf_op jit(solution)/shard_map/ppermute | solution.py:28
  73.3 3.6 %collective-permute-done.5 = f32[3,1,8,128]{3,2,1,0:T(8,128)S(1)} collective-permute-done((f32[3,1,8,128]{3,2,1,0:T(8,128)S(1)}, f32[3,1,8,128]{3,2,1,0:T(8,128)S(1)}, u32[]{:S(2)}, u32[]{:S(2)}) %collective-permute-start.5) | collective-permute-done | bytes 12320 | tf_op jit(solution)/shard_map/ppermute | solution.py:26
  78.4 2.7 %collective-permute-done.7 = f32[3,10,1,128]{3,2,1,0:T(1,128)S(1)} collective-permute-done((f32[3,10,1,128]{3,2,1,0:T(1,128)S(1)}, f32[3,10,1,128]{3,2,1,0:T(1,128)S(1)}, u32[]{:S(2)}, u32[]{:S(2)}) %collective-permute-start.7) | collective-permute-done | bytes 15392 | tf_op jit(solution)/shard_map/ppermute | solution.py:26
  81.2 0.8 reshape.260
  83.7 8.6 %all_to_all.16 = f32[16,2,1536]{2,1,0:T(2,128)S(1)} all-to-all(f32[16,2,1536]{2,1,0:T(2,128)S(1)} %select_multiply_fusion), channel_id=1, replica_groups=mesh['gy'=4,'gz'=8] {'gz'}, dimensions={0} | all-to-all | bytes 393216 | tf_op jit(solution)/shard_map/all_to_all | solution.py:177
  92.7 1.0 %fusion.2 = f32[8,3,128]{2,1,0:T(4,128)} fusion(f32[8,2,3,8,64]{4,3,2,0,1:T(8,128)S(1)} %reshape.262, f32[8,8,128]{2,1,0:T(8,128)S(1)} %get-tuple-element.31, f32[8,8,128]{2,1,0:T(8,128)S(1)} %get-tuple-element.30, f32[8,2,128]{2,1,0:T(2,128)S(1)} %compare_convert_fusion, f32[8,8,128]{2,1,0:T(8,128)S(1)} %get-tuple-element.29), kind=kOutput, calls=%fused_computation.7 | convolution fusion | flops 37958656 | bytes 217088 | tf_op jit(solution)/shard_map/bkcjn,bnm->bkcjm/dot_general | solution.py:73
  (80 shorter events, 10.0 us)
Async XLA Ops:
  4.4 52.4 %all-to-all-start = ((s32[8,2,2]{1,2,0:T(2,128)}), s32[8,2,2]{1,2,0:T(2,128)S(1)}, u32[]{:S(2)}, u32[]{:S(2)}) async-start(s32[8,2,2]{1,2,0:T(2,128)} %copy.81), calls=%async_computation | async-start | bytes 16384 | tf_op jit(solution)/shard_map/all_to_all | solution.py:162
  10.4 51.0 %collective-permute-start.1 = (f32[3,1,8,128]{3,2,1,0:T(8,128)S(1)}, f32[3,1,8,128]{3,2,1,0:T(8,128)S(1)}, u32[]{:S(2)}, u32[]{:S(2)}) collective-permute-start(f32[3,1,8,128]{3,2,1,0:T(8,128)S(1)} %get-tuple-element.16), channel_id=1, source_target_pairs={{0,8},{8,16},{16,24},{24,0},{1,9},{9,17},{17,25},{25,1},{2,10},{10... | collective-permute-start | bytes 36872 | tf_op jit(solution)/shard_map/ppermute | solution.py:26
  11.9 49.5 %collective-permute-start = (f32[3,1,8,128]{3,2,1,0:T(8,128)S(1)}, f32[3,1,8,128]{3,2,1,0:T(8,128)S(1)}, u32[]{:S(2)}, u32[]{:S(2)}) collective-permute-start(f32[3,1,8,128]{3,2,1,0:T(8,128)S(1)} %get-tuple-element.15), channel_id=1, source_target_pairs={{8,0},{16,8},{24,16},{0,24},{9,1},{17,9},{25,17},{1,25},{10,2},{18... | collective-permute-start | bytes 36872 | tf_op jit(solution)/shard_map/ppermute | solution.py:28
  54.3 7.0 %copy-start = (f32[3,8,8,128]{3,2,1,0:T(8,128)S(1)}, f32[3,8,8,128]{3,2,1,0:T(8,128)}, u32[]{:S(2)}) copy-start(f32[3,8,8,128]{3,2,1,0:T(8,128)} %param.8) | copy-start | bytes 294916
  56.8 10.4 %all-to-all-start.1 = ((f32[16,2,1536]{2,1,0:T(2,128)}), f32[16,2,1536]{2,1,0:T(2,128)S(1)}, u32[]{:S(2)}, u32[]{:S(2)}) async-start(f32[16,2,1536]{2,1,0:T(2,128)} %copy.91), calls=%async_computation.1 | async-start | bytes 393216 | tf_op jit(solution)/shard_map/all_to_all | solution.py:161
  61.4 8.0 %collective-permute-start.2 = (f32[3,10,1,128]{3,2,1,0:T(1,128)S(1)}, f32[3,10,1,128]{3,2,1,0:T(1,128)S(1)}, u32[]{:S(2)}, u32[]{:S(2)}) collective-permute-start(f32[3,10,1,128]{3,2,1,0:T(1,128)S(1)} %get-tuple-element.11), channel_id=1, source_target_pairs={{1,0},{2,1},{3,2},{4,3},{5,4},{6,5},{7,6},{0,7},{9,8},{10,9},{11,1... | collective-permute-start | bytes 46088 | tf_op jit(solution)/shard_map/ppermute | solution.py:28
  64.1 5.3 %collective-permute-start.3 = (f32[3,10,1,128]{3,2,1,0:T(1,128)S(1)}, f32[3,10,1,128]{3,2,1,0:T(1,128)S(1)}, u32[]{:S(2)}, u32[]{:S(2)}) collective-permute-start(f32[3,10,1,128]{3,2,1,0:T(1,128)S(1)} %get-tuple-element.12), channel_id=1, source_target_pairs={{0,1},{1,2},{2,3},{3,4},{4,5},{5,6},{6,7},{7,0},{8,9},{9,10},{10,1... | collective-permute-start | bytes 46088 | tf_op jit(solution)/shard_map/ppermute | solution.py:26
  69.6 3.7 %collective-permute-start.4 = (f32[3,1,8,128]{3,2,1,0:T(8,128)S(1)}, f32[3,1,8,128]{3,2,1,0:T(8,128)S(1)}, u32[]{:S(2)}, u32[]{:S(2)}) collective-permute-start(f32[3,1,8,128]{3,2,1,0:T(8,128)S(1)} %get-tuple-element.14), channel_id=1, source_target_pairs={{8,0},{16,8},{24,16},{0,24},{9,1},{17,9},{25,17},{1,25},{10,2},{18... | collective-permute-start | bytes 36872 | tf_op jit(solution)/shard_map/ppermute | solution.py:28
  71.4 5.5 %collective-permute-start.5 = (f32[3,1,8,128]{3,2,1,0:T(8,128)S(1)}, f32[3,1,8,128]{3,2,1,0:T(8,128)S(1)}, u32[]{:S(2)}, u32[]{:S(2)}) collective-permute-start(f32[3,1,8,128]{3,2,1,0:T(8,128)S(1)} %get-tuple-element.13), channel_id=1, source_target_pairs={{0,8},{8,16},{16,24},{24,0},{1,9},{9,17},{17,25},{25,1},{2,10},{10... | collective-permute-start | bytes 36872 | tf_op jit(solution)/shard_map/ppermute | solution.py:26
  76.9 1.5 %collective-permute-start.6 = (f32[3,10,1,128]{3,2,1,0:T(1,128)S(1)}, f32[3,10,1,128]{3,2,1,0:T(1,128)S(1)}, u32[]{:S(2)}, u32[]{:S(2)}) collective-permute-start(f32[3,10,1,128]{3,2,1,0:T(1,128)S(1)} %get-tuple-element.9), channel_id=1, source_target_pairs={{1,0},{2,1},{3,2},{4,3},{5,4},{6,5},{7,6},{0,7},{9,8},{10,9},{11,1... | collective-permute-start | bytes 46088 | tf_op jit(solution)/shard_map/ppermute | solution.py:28
  77.0 4.1 %collective-permute-start.7 = (f32[3,10,1,128]{3,2,1,0:T(1,128)S(1)}, f32[3,10,1,128]{3,2,1,0:T(1,128)S(1)}, u32[]{:S(2)}, u32[]{:S(2)}) collective-permute-start(f32[3,10,1,128]{3,2,1,0:T(1,128)S(1)} %get-tuple-element.10), channel_id=1, source_target_pairs={{0,1},{1,2},{2,3},{3,4},{4,5},{5,6},{6,7},{7,0},{8,9},{9,10},{10,1... | collective-permute-start | bytes 46088 | tf_op jit(solution)/shard_map/ppermute | solution.py:26
  81.2 1.3 %copy-start.1 = (f32[3,8,8,128]{3,2,1,0:T(8,128)}, f32[3,8,8,128]{3,2,1,0:T(8,128)S(1)}, u32[]{:S(2)}) copy-start(f32[3,8,8,128]{3,2,1,0:T(8,128)S(1)} %fusion.27) | copy-start | bytes 294916
where the time goes:
time: 94.3 us; the launch traced here: 93.8 us
  local copies, waits for them, and re-layouts  45.2 us (48%)
  starting transfers between devices  18.6 us (20%)
  waiting for transfers between devices  11.4 us (12%)
  blocking collectives  8.6 us (9%)
  other arithmetic  6.25 us (7%)
  matrix products  2.76 us (3%)
  between operations  1.02 us (1%)
    gather x8, local copies, waits for them, and re-layouts, fibre_force(): delta = jnp.take_along_axis(position, partner_index, axis=2) - position  37 us
    all_to_all x1, blocking collectives, local(): lax.all_to_all(tile_values, 'gz', split_axis=0, concat_axis=0, tiled=True)  8.6 us
    ppermute x4, starting transfers between devices, padded_2(): lax.ppermute(head, axis, [((i + 1) % count, i) for i in range(count)])  6.86 us
    ppermute x4, waiting for transfers between devices, padded_2(): lax.ppermute(tail, axis, [(i, (i + 1) % count) for i in range(count)])  6.28 us
    all_to_all x1, starting transfers between devices, local(): lax.all_to_all(sent_tiles, 'gz', split_axis=0, concat_axis=0, tiled=True)  5.2 us
    all_to_all x1, starting transfers between devices, local(): lax.all_to_all(outgoing, 'gz', split_axis=0, concat_axis=0, tiled=True)  4.2 us
    all_to_all x1, waiting for transfers between devices, local(): lax.all_to_all(outgoing, 'gz', split_axis=0, concat_axis=0, tiled=True)  3.07 us
    ppermute x4, starting transfers between devices, padded_2(): lax.ppermute(tail, axis, [(i, (i + 1) % count) for i in range(count)])  2.3 us
  transfers between devices with their start and end apart: 10, of which 5 were waited for; matrix products, arithmetic and copies ran while one was open for 49% of the time, Pallas kernels for 0%

commit v1 on v0

v1 whole, which is shorter than its diff:
```python
import functools
import math

import jax
import jax.numpy as jnp
from jax import lax
from jax.experimental import pallas as pl
from jax.experimental.pallas import tpu as pltpu
from jax.sharding import PartitionSpec as P

BLOCK = 128
SIDE = 8
VISCOUS = 0.125
FORCING = 0.5
MESH = pl.DeviceIdType.MESH
F32 = jnp.float32
BF16 = jnp.bfloat16


def split(x):
    hi = x.astype(BF16)
    return hi, (x - hi.astype(F32)).astype(BF16)


def cos_sin(offset):
    u = jnp.floor(offset + 0.5)
    a = (offset - u) * (0.5 * math.pi)
    u = u - 4.0
    z = a * a
    s = a * (1.0 + z * (-1 / 6 + z * (1 / 120 + z * (-1 / 5040 + z * (1 / 362880)))))
    c = 1.0 + z * (-0.5 + z * (1 / 24 + z * (-1 / 720 + z * (1 / 40320 - z * (1 / 3628800)))))
    w = jnp.abs(u)
    cq = 1.0 - w
    sq = u * (2.0 - w)
    return cq * c - sq * s, sq * c + cq * s


def diffuse(f, ylo, yhi, zlo, zhi):
    shape = f.shape
    z = lax.broadcasted_iota(jnp.int32, shape, 2)
    x = lax.broadcasted_iota(jnp.int32, shape, 3)
    y_down = jnp.concatenate([ylo, f[:, :-1]], axis=1)
    y_up = jnp.concatenate([f[:, 1:], yhi], axis=1)
    z_down = jnp.where(z == 0, jnp.broadcast_to(zlo, shape), pltpu.roll(f, 1, 2))
    z_up = jnp.where(z == shape[2] - 1, jnp.broadcast_to(zhi, shape), pltpu.roll(f, shape[2] - 1, 2))
    x_down = jnp.where(x == 0, 0.0, pltpu.roll(f, 1, 3))
    x_up = jnp.where(x == shape[3] - 1, 0.0, pltpu.roll(f, shape[3] - 1, 3))
    beside = (y_down + y_up) + (z_down + z_up) + (x_down + x_up)
    return f + VISCOUS * (beside - 6.0 * f)


def kernel(
    rows, peers, cap,
    v_ref, off_ref, slot_ref, link_ref, owner_ref, tile_ref,
    nv_ref, mv_ref,
    stage, sendb, recvb, px_ref, w_ref, retsend, retrecv, f1_ref, hy, hz, gy_, gz_,
    m_send, m_recv, r_send, r_recv, h_send, h_recv, g_send, g_recv,
):
    me_y, me = lax.axis_index("gy"), lax.axis_index("gz")
    y_next, y_prev = lax.rem(me_y + 1, rows), lax.rem(me_y + rows - 1, rows)
    z_next, z_prev = lax.rem(me + 1, peers), lax.rem(me + peers - 1, peers)
    ahead = [lax.rem(me + d, peers) for d in range(peers)]
    behind = [lax.rem(me + peers - d, peers) for d in range(peers)]
    nb = owner_ref.shape[0]
    nx = v_ref.shape[3]

    barrier = pltpu.get_barrier_semaphore()
    for d in range(1, peers):
        pl.semaphore_signal(barrier, inc=1, device_id=(me_y, ahead[d]), device_id_type=MESH)
    for other in (y_next, y_prev):
        pl.semaphore_signal(barrier, inc=1, device_id=(other, me), device_id_type=MESH)

    def by_block(ref, row):
        return jnp.concatenate(
            [ref[row : row + 1, b * BLOCK : (b + 1) * BLOCK] for b in range(nb)], axis=0
        )

    offs = [by_block(off_ref, r) for r in range(3)]
    owner = jnp.broadcast_to(owner_ref[...], (nb, BLOCK))
    tile_x = jnp.where(
        slot_ref[...] == 0,
        jnp.broadcast_to(tile_ref[:, 0:1], (nb, BLOCK)),
        jnp.broadcast_to(tile_ref[:, 1:2], (nb, BLOCK)),
    )
    first_x = (tile_x * SIDE).astype(F32)
    position = [
        (me_y * SIDE).astype(F32) + offs[0],
        (owner * SIDE).astype(F32) + offs[1],
        first_x + offs[2],
    ]
    force = [jnp.zeros((nb, BLOCK), F32) for _ in range(3)]
    for side in range(2):
        partner = by_block(link_ref, side)
        delta = [
            jnp.take_along_axis(p, partner, axis=1, mode="promise_in_bounds") - p for p in position
        ]
        length = jnp.sqrt(delta[0] * delta[0] + delta[1] * delta[1] + delta[2] * delta[2])
        scale = jnp.maximum(length, 1.0)
        force = [f + dl / scale for f, dl in zip(force, delta)]
    sub = lax.broadcasted_iota(jnp.int32, (nb, BLOCK), 0)
    rank = jnp.zeros((nb, BLOCK), jnp.int32)
    for b in range(nb - 1):
        same = jnp.broadcast_to(owner[b : b + 1], (nb, BLOCK)) == owner
        rank = rank + jnp.where(same & (sub > b), 1, 0)
    key = owner * cap + rank

    for r, row in enumerate(offs + [first_x] + force + [jnp.zeros((nb, BLOCK), F32)]):
        stage[r] = row
    blocks = [stage[:, b, :] for b in range(nb)]
    keys = [jnp.broadcast_to(key[b : b + 1], (8, BLOCK)) for b in range(nb)]
    for d in range(peers):
        for k in range(cap):
            acc = jnp.zeros((8, BLOCK), F32)
            for b in range(nb):
                acc = jnp.where(keys[b] == ahead[d] * cap + k, blocks[b], acc)
            if d == 0:
                recvb[0, k] = acc
            else:
                sendb[d, k] = acc

    def faces(src, ybuf, zbuf, send, recv):
        last = SIDE - 1
        pairs = [
            (src.at[:, pl.ds(last, 1)], ybuf.at[:, pl.ds(0, 1)], (y_next, me)),
            (src.at[:, pl.ds(0, 1)], ybuf.at[:, pl.ds(1, 1)], (y_prev, me)),
            (src.at[:, :, pl.ds(last, 1)], zbuf.at[:, :, pl.ds(last, 1)], (me_y, z_next)),
            (src.at[:, :, pl.ds(0, 1)], zbuf.at[:, :, pl.ds(0, 1)], (me_y, z_prev)),
        ]
        return [
            pltpu.make_async_remote_copy(
                src_ref=a, dst_ref=b, send_sem=send.at[i], recv_sem=recv.at[i],
                device_id=to, device_id_type=MESH,
            )
            for i, (a, b, to) in enumerate(pairs)
        ]

    def layers(ybuf, zbuf):
        last = SIDE - 1
        return ybuf[:, 0:1], ybuf[:, 1:2], zbuf[:, :, last : last + 1], zbuf[:, :, 0:1]

    pl.semaphore_wait(barrier, peers + 1)
    outgoing = []
    for d in range(1, peers):
        copy = pltpu.make_async_remote_copy(
            src_ref=sendb.at[d], dst_ref=recvb.at[d], send_sem=m_send.at[d], recv_sem=m_recv.at[d],
            device_id=(me_y, ahead[d]), device_id_type=MESH,
        )
        copy.start()
        outgoing.append(copy)
    halo = faces(v_ref, hy, hz, h_send, h_recv)
    for copy in halo:
        copy.start()

    cell = lax.broadcasted_iota(jnp.int32, (SIDE, BLOCK), 0)
    cell_f = cell.astype(F32)
    quarter = cell % 4
    cos_cell = jnp.where(quarter == 0, 0.25, jnp.where(quarter == 2, -0.25, 0.0))
    sin_cell = jnp.where(quarter == 1, 0.25, jnp.where(quarter == 3, -0.25, 0.0))
    wide = jnp.zeros((3 * SIDE * SIDE, 2 * nx), F32)
    narrow = jnp.zeros((3 * SIDE * SIDE, nx), F32)
    nt = (((1,), (1,)), ((), ()))
    for d in range(peers):
        if d > 0:
            outgoing[d - 1].wait_recv()
        his, los = [], []
        for k in range(cap):
            data = recvb[d, k]
            cosines, sines = cos_sin(data)
            weights = []
            for r in range(3):
                near = jnp.abs(cell_f - data[r : r + 1]) < 2.0
                bump = 0.25 + (cos_cell * cosines[r : r + 1] + sin_cell * sines[r : r + 1])
                weights.append(jnp.where(near, bump, 0.0))
            wy, wz, wx = weights
            plane = jnp.concatenate([wy[y : y + 1] * wz for y in range(SIDE)], axis=0)
            w_ref[d, k] = plane
            lifted = jnp.concatenate([data[4 + c : 5 + c] * plane for c in range(3)], axis=0)
            hi, lo = split(lifted)
            his.append(hi)
            los.append(lo)
            wx_hi = wx.astype(BF16).astype(F32)
            wx_lo = wx - wx_hi
            start = jnp.broadcast_to(data[3:4], (SIDE, BLOCK))
            spots = [start == float(SIDE * t) for t in range(nx // SIDE)]
            for part, piece in enumerate((wx_hi, wx_lo)):
                full = jnp.concatenate([jnp.where(s, piece, 0.0) for s in spots], axis=0)
                px_ref[d, part * nx : (part + 1) * nx, k * BLOCK : (k + 1) * BLOCK] = full.astype(BF16)
        hi = jnp.concatenate(his, axis=1)
        lo = jnp.concatenate(los, axis=1)
        wide = wide + lax.dot_general(hi, px_ref[d], nt, preferred_element_type=F32)
        narrow = narrow + lax.dot_general(lo, px_ref[d, :nx], nt, preferred_element_type=F32)
    spread = (FORCING * (wide[:, :nx] + (wide[:, nx:] + narrow))).reshape(3, SIDE, SIDE, nx)

    for copy in halo:
        copy.wait_recv()
    f1 = diffuse(v_ref[...], *layers(hy, hz)) + spread
    f1_ref[...] = f1
    halo1 = faces(f1_ref, gy_, gz_, g_send, g_recv)
    for copy in halo1:
        copy.start()
    for copy in halo1:
        copy.wait_recv()
    f2 = diffuse(f1, *layers(gy_, gz_)) + spread
    nv_ref[...] = f2

    hi, lo = split(f2.reshape(3 * SIDE * SIDE, nx))
    hihi = jnp.concatenate([hi, hi], axis=1)
    back = []
    for d in list(range(1, peers)) + [0]:
        got = jnp.dot(hihi, px_ref[d], preferred_element_type=F32) + jnp.dot(
            lo, px_ref[d, :nx], preferred_element_type=F32
        )
        lines = []
        for k in range(cap):
            plane = w_ref[d, k]
            for c in range(3):
                part = got[c * 64 : (c + 1) * 64, k * BLOCK : (k + 1) * BLOCK] * plane
                lines.append(jnp.sum(part, axis=0, keepdims=True))
        lines.append(jnp.zeros((8 - 3 * cap, BLOCK), F32))
        result = jnp.concatenate(lines, axis=0)
        if d == 0:
            retrecv[0] = result
        else:
            retsend[d] = result
            copy = pltpu.make_async_remote_copy(
                src_ref=retsend.at[d], dst_ref=retrecv.at[d],
                send_sem=r_send.at[d], recv_sem=r_recv.at[d],
                device_id=(me_y, behind[d]), device_id_type=MESH,
            )
            copy.start()
            back.append(copy)
    for copy in back:
        copy.wait_recv()
    arrived = [retrecv[d] for d in range(peers)]
    for b in range(nb):
        mine = jnp.broadcast_to(owner[b : b + 1], (8, BLOCK))
        acc = jnp.zeros((8, BLOCK), F32)
        for d in range(peers):
            acc = jnp.where(mine == ahead[d], arrived[d], acc)
        second = jnp.broadcast_to(rank[b : b + 1], (3, BLOCK)) == 1
        mv_ref[:, b * BLOCK : (b + 1) * BLOCK] = jnp.where(second, acc[3:6], acc[0:3])
    for copy in outgoing + halo + halo1 + back:
        copy.wait_send()


def local(rows, peers, velocity, offsets, marker_slot, fibre_links, block_owner, block_tiles):
    nb = block_owner.shape[0]
    cap = max(2, 2 * nb // peers)
    nx = velocity.shape[3]
    assert velocity.shape[1:3] == (SIDE, SIDE) and nb == 8 and cap == 2
    vmem = pl.BlockSpec(memory_space=pltpu.VMEM)
    dma = pltpu.SemaphoreType.DMA
    return pl.pallas_call(
        functools.partial(kernel, rows, peers, cap),
        out_shape=(
            jax.ShapeDtypeStruct(velocity.shape, F32),
            jax.ShapeDtypeStruct(offsets.shape, F32),
        ),
        in_specs=[vmem] * 6,
        out_specs=(vmem, vmem),
        scratch_shapes=[
            pltpu.VMEM((8, nb, BLOCK), F32),
            pltpu.VMEM((peers, cap, 8, BLOCK), F32),
            pltpu.VMEM((peers, cap, 8, BLOCK), F32),
            pltpu.VMEM((peers, 2 * nx, cap * BLOCK), BF16),
            pltpu.VMEM((peers, cap, SIDE * SIDE, BLOCK), F32),
            pltpu.VMEM((peers, 8, BLOCK), F32),
            pltpu.VMEM((peers, 8, BLOCK), F32),
            pltpu.VMEM((3, SIDE, SIDE, nx), F32),
            pltpu.VMEM((3, 2, SIDE, nx), F32),
            pltpu.VMEM((3, SIDE, SIDE, nx), F32),
            pltpu.VMEM((3, 2, SIDE, nx), F32),
            pltpu.VMEM((3, SIDE, SIDE, nx), F32),
            dma((peers,)), dma((peers,)), dma((peers,)), dma((peers,)),
            dma((4,)), dma((4,)), dma((4,)), dma((4,)),
        ],
        compiler_params=pltpu.CompilerParams(collective_id=0, has_side_effects=True),
    )(
        velocity, offsets, marker_slot.reshape(nb, BLOCK), fibre_links, block_owner, block_tiles
    )


def solution(mesh):
    return jax.shard_map(
        functools.partial(local, mesh.shape["gy"], mesh.shape["gz"]),
        mesh=mesh,
        in_specs=(
            P(None, "gy", "gz", None),
            P(None, ("gy", "gz")),
            P(("gy", "gz")),
            P(None, ("gy", "gz")),
            P(("gy", "gz"), None),
            P(("gy", "gz"), None),
        ),
        out_specs=(P(None, "gy", "gz", None), P(None, ("gy", "gz"))),
        check_vma=False,
    )
```

time: 94.3 us -> 25.2 us (0.27)
  local copies, waits for them, and re-layouts: 45.2 us -> 4.15 us
  Pallas kernels: 0 us -> 20.2 us
  starting transfers between devices: 18.6 us -> 0 us
  waiting for transfers between devices: 11.4 us -> 0 us
  blocking collectives: 8.6 us -> 0 us
  other arithmetic: 6.25 us -> 0 us
  matrix products: 2.76 us -> 0 us
    gather x10 -> x0, local copies, waits for them, and re-layouts: 37.7 us -> none  [the longest x8 37 us: fibre_force(): delta = jnp.take_along_axis(position, partner_index, axis=2) - position]
    pallas_call x0 -> x1, Pallas kernels: none -> 20.2 us  [local(): pl.pallas_call(functools.partial(kernel, rows, peers, cap), out_shape=(ja...]
    all_to_all x2 -> x0, starting transfers between devices: 9.4 us -> none  [the longest x1 5.2 us: local(): lax.all_to_all(sent_tiles, 'gz', split_axis=0, concat_axis=0, tiled=True)]
    ppermute x8 -> x0, starting transfers between devices: 9.15 us -> none  [the longest x4 6.86 us: padded_2(): lax.ppermute(head, axis, [((i + 1) % count, i) for i in range(count)])]
    all_to_all x1 -> x0, blocking collectives: 8.6 us -> none  [local(): lax.all_to_all(tile_values, 'gz', split_axis=0, concat_axis=0, tiled=True)]
    ppermute x8 -> x0, waiting for transfers between devices: 8.3 us -> none  [the longest x4 6.28 us: padded_2(): lax.ppermute(tail, axis, [(i, (i + 1) % count) for i in range(count)])]
    unnamed x6 -> x10, local copies, waits for them, and re-layouts: 0.03 us -> 4.15 us
    all_to_all x2 -> x0, waiting for transfers between devices: 3.07 us -> none  [the longest x1 3.07 us: local(): lax.all_to_all(outgoing, 'gz', split_axis=0, concat_axis=0, tiled=True)]
  transfers between devices with their start and end apart: 10 -> 0, of which waited for: 5 -> 0; matrix products, arithmetic and copies ran while one was open for 49% -> 0% of each run, Pallas kernels for 0% -> 0%
where the time goes in v1:
time: 25.2 us; the launch traced here: 25 us
  Pallas kernels  20.2 us (80%)
  local copies, waits for them, and re-layouts  4.15 us (16%)
  between operations  0.66 us (3%)
    pallas_call x1, Pallas kernels, local(): pl.pallas_call(functools.partial(kernel, rows, peers, cap), out_shape=(ja...  20.2 us
    unnamed x10, local copies, waits for them, and re-layouts  4.15 us

profile of v1, /device:TPU:0, one launch (start us, length us, event | category | flops | bytes accessed | tf_op | source)
XLA Modules:
  0.0 25.0 jit_solution(14900372350103509668)
XLA Ops:
  0.6 0.0 copy-start.2
  0.6 0.6 %copy-done.2 = s32[8,1]{0,1:T(1,128)S(1)} copy-done((s32[8,1]{0,1:T(1,128)S(1)}, s32[8,1]{0,1:T(1,128)}, u32[]{:S(2)}) %copy-start.2) | copy-done | bytes 56
  1.3 0.0 copy-start.1
  1.3 0.7 %copy.8.owner_ref = s32[8,1]{1,0:T(8,128)} copy(s32[8,1]{0,1:T(1,128)S(1)} %copy-done.2) | data formatting | bytes 64 | tf_op args[4]
  2.0 0.0 copy-done.1
  2.0 0.7 %copy.9.tile_ref = s32[8,2]{1,0:T(8,128)} copy(s32[8,2]{0,1:T(2,128)S(1)} %copy-done.1) | data formatting | bytes 128 | tf_op args[5]
  2.6 20.2 %shard_map.77 = (f32[3,8,8,128]{3,2,1,0:T(8,128)}, f32[3,1024]{1,0:T(4,128)}) custom-call(f32[3,8,8,128]{3,2,1,0:T(8,128)} %v_ref.1, f32[3,1024]{1,0:T(4,128)} %off_ref.1, s32[8,128]{1,0:T(8,128)} %bitcast.1, s32[2,1024]{1,0:T(2,128)} %link_ref.1, s32[8,1]{1,0:T(8,128)} %copy.8.owner_ref, s32[8,2]{1,0:T(8,128)} %copy.9.tile_ref), custom_call_target="tpu_custom_call" | custom-call | tf_op jit(solution)/shard_map/pallas_call | solution.py:253
  22.8 0.0 copy-start
  22.8 1.5 %copy.12 = f32[3,8,8,128]{3,2,1,0:T(8,128)} copy(f32[3,8,8,128]{3,2,1,0:T(8,128)} %get-tuple-element.4) | data formatting | bytes 196608
  24.4 0.0 copy-done
  24.4 0.6 %copy.13 = f32[3,1024]{1,0:T(4,128)} copy(f32[3,1024]{1,0:T(4,128)S(1)} %copy-done) | data formatting | bytes 24576
Async XLA Ops:
  0.6 0.7 %copy-start.2 = (s32[8,1]{0,1:T(1,128)S(1)}, s32[8,1]{0,1:T(1,128)}, u32[]{:S(2)}) copy-start(s32[8,1]{0,1:T(1,128)} %param.10) | copy-start | bytes 100
  1.3 0.7 %copy-start.1 = (s32[8,2]{0,1:T(2,128)S(1)}, s32[8,2]{0,1:T(2,128)}, u32[]{:S(2)}) copy-start(s32[8,2]{0,1:T(2,128)} %param.11) | copy-start | bytes 196
  22.8 1.6 %copy-start = (f32[3,1024]{1,0:T(4,128)S(1)}, f32[3,1024]{1,0:T(4,128)}, u32[]{:S(2)}) copy-start(f32[3,1024]{1,0:T(4,128)} %get-tuple-element.5) | copy-start | bytes 36868

commit v2 on v1

--- a/solution.py
+++ b/solution.py
@@ -61,7 +61,7 @@
     z_next, z_prev = lax.rem(me + 1, peers), lax.rem(me + peers - 1, peers)
     ahead = [lax.rem(me + d, peers) for d in range(peers)]
     behind = [lax.rem(me + peers - d, peers) for d in range(peers)]
-    nb = owner_ref.shape[0]
+    nb = owner_ref.shape[1]
     nx = v_ref.shape[3]
 
     barrier = pltpu.get_barrier_semaphore()
@@ -75,12 +75,21 @@
             [ref[row : row + 1, b * BLOCK : (b + 1) * BLOCK] for b in range(nb)], axis=0
         )
 
+    own_row = lax.broadcasted_iota(jnp.int32, (nb, nb), 0) == lax.broadcasted_iota(
+        jnp.int32, (nb, nb), 1
+    )
+
+    def column(row):
+        spread_row = jnp.broadcast_to(row.astype(F32), (nb, nb))
+        total = jnp.sum(jnp.where(own_row, spread_row, 0.0), axis=1, keepdims=True)
+        return jnp.broadcast_to(total, (nb, BLOCK)).astype(jnp.int32)
+
     offs = [by_block(off_ref, r) for r in range(3)]
-    owner = jnp.broadcast_to(owner_ref[...], (nb, BLOCK))
+    owner = column(owner_ref[...])
     tile_x = jnp.where(
         slot_ref[...] == 0,
-        jnp.broadcast_to(tile_ref[:, 0:1], (nb, BLOCK)),
-        jnp.broadcast_to(tile_ref[:, 1:2], (nb, BLOCK)),
+        column(tile_ref[0:1]),
+        column(tile_ref[1:2]),
     )
     first_x = (tile_x * SIDE).astype(F32)
     position = [
@@ -160,6 +169,10 @@
     narrow = jnp.zeros((3 * SIDE * SIDE, nx), F32)
     nt = (((1,), (1,)), ((), ()))
     for d in range(peers):
+        if d == 1:
+            for copy in halo:
+                copy.wait_recv()
+            f1_ref[...] = diffuse(v_ref[...], *layers(hy, hz))
         if d > 0:
             outgoing[d - 1].wait_recv()
         his, los = [], []
@@ -191,9 +204,7 @@
         narrow = narrow + lax.dot_general(lo, px_ref[d, :nx], nt, preferred_element_type=F32)
     spread = (FORCING * (wide[:, :nx] + (wide[:, nx:] + narrow))).reshape(3, SIDE, SIDE, nx)
 
-    for copy in halo:
-        copy.wait_recv()
-    f1 = diffuse(v_ref[...], *layers(hy, hz)) + spread
+    f1 = f1_ref[...] + spread
     f1_ref[...] = f1
     halo1 = faces(f1_ref, gy_, gz_, g_send, g_recv)
     for copy in halo1:
@@ -276,7 +287,7 @@
         ],
         compiler_params=pltpu.CompilerParams(collective_id=0, has_side_effects=True),
     )(
-        velocity, offsets, marker_slot.reshape(nb, BLOCK), fibre_links, block_owner, block_tiles
+        velocity, offsets, marker_slot.reshape(nb, BLOCK), fibre_links, block_owner.T, block_tiles.T
     )
 
 

time: 25.2 us -> 24.5 us (0.972)
  local copies, waits for them, and re-layouts: 4.15 us -> 2.15 us
  Pallas kernels: 20.2 us -> 21.5 us
    unnamed x10 -> x4, local copies, waits for them, and re-layouts: 4.15 us -> 2.15 us
    pallas_call x1, Pallas kernels: 20.2 us -> 21.5 us  [local(): pl.pallas_call(functools.partial(kernel, rows, peers, cap), out_shape=(ja...]
where the time goes in v2:
time: 24.5 us; the launch traced here: 24.3 us
  Pallas kernels  21.5 us (88%)
  local copies, waits for them, and re-layouts  2.15 us (9%)
  between operations  0.65 us (3%)
    pallas_call x1, Pallas kernels, local(): pl.pallas_call(functools.partial(kernel, rows, peers, cap), out_shape=(ja...  21.5 us
    unnamed x4, local copies, waits for them, and re-layouts  2.15 us

profile of v2, /device:TPU:0, one launch (start us, length us, event | category | flops | bytes accessed | tf_op | source)
XLA Modules:
  0.0 24.3 jit_solution(8471641536807533976)
XLA Ops:
  0.6 21.5 %shard_map.77 = (f32[3,8,8,128]{3,2,1,0:T(8,128)}, f32[3,1024]{1,0:T(4,128)}) custom-call(f32[3,8,8,128]{3,2,1,0:T(8,128)} %v_ref.1, f32[3,1024]{1,0:T(4,128)} %off_ref.1, s32[8,128]{1,0:T(8,128)} %bitcast.3, s32[2,1024]{1,0:T(2,128)} %link_ref.1, s32[1,8]{1,0:T(1,128)} %bitcast.5, s32[2,8]{1,0:T(2,128)} %bitcast.4), custom_call_target="tpu_custom_call" | custom-call | tf_op jit(solution)/shard_map/pallas_call | solution.py:264
  22.1 0.0 copy-start
  22.1 1.5 %copy.10 = f32[3,8,8,128]{3,2,1,0:T(8,128)} copy(f32[3,8,8,128]{3,2,1,0:T(8,128)} %get-tuple-element.4) | data formatting | bytes 196608
  23.7 0.0 copy-done
  23.7 0.6 %copy.11 = f32[3,1024]{1,0:T(4,128)} copy(f32[3,1024]{1,0:T(4,128)S(1)} %copy-done) | data formatting | bytes 24576
Async XLA Ops:
  22.1 1.6 %copy-start = (f32[3,1024]{1,0:T(4,128)S(1)}, f32[3,1024]{1,0:T(4,128)}, u32[]{:S(2)}) copy-start(f32[3,1024]{1,0:T(4,128)} %get-tuple-element.5) | copy-start | bytes 36868
